TPU v7x, 32 devices: a whole 2x2x4 slice. The times are simulated.
32 devices in a mesh: tx: 2 (over core), ty: 4 (over y, x), lz: 4 (over z).
Axes of the slice: x: 2, y: 2, z: 4, core: 2. Of those that a mesh axis runs over, the one named last changes fastest.
Arguments:
- test_field: bfloat16 [64, 6, 48, 512], P('tx', None, 'lz', 'ty'), may hold values from -6 to 6
- dir_field: bfloat16 [64, 6, 48, 512], P('tx', None, 'lz', 'ty'), may hold values from -6 to 6
- border_b: bfloat16 [64, 6, 48, 512], P('tx', None, 'lz', 'ty')
- border_c: bfloat16 [64, 6, 48, 512], P('tx', None, 'lz', 'ty')
- land_mask: int32 [64, 512], P('tx', 'ty'), may hold values from 0 to 1, as said below
- active_rows: int32 [64, 4], P('tx', 'ty'), may hold values from -1 to 31, as said below
- cell_blocks: bfloat16 [64, 36, 512], P('tx', None, 'ty'), may hold values from -2.5 to 2.5
- column_k: bfloat16 [288, 288], replicated, may hold values from -0.375 to 0.375
- kappa: float32 [6], replicated, may hold values from 0.2 to 1
Outputs:
- test_image: bfloat16 [64, 6, 48, 512], P('tx', None, 'lz', 'ty')
- dir_image: bfloat16 [64, 6, 48, 512], P('tx', None, 'lz', 'ty')
- border: float32 [3], replicated
Inputs may be any that keep to these rules, and one draw needn't show every extreme that they name: `active_rows`: in each tile the 32 entries name distinct local rows, the active ones, followed by -1 for the rest; some tile has all 32 rows active. `land_mask`: cells whose latitude index y has y % 128 equal to 0 or 127 are ocean.
All inputs are finite; a program needn't handle non-finite values.
Results may differ from a plain program's by a relative error of at most 0.0028.
Values may be sent and summed in bfloat16 or wider, within the bound.
A program may use at most 192 MiB of HBM per device.

v0:
```python
import jax
import jax.numpy as jnp
from jax import lax
from jax.sharding import PartitionSpec as P


def extended(value, sides, width, wrap):
    for axis, dim in sides:
        size, length = (lax.axis_size(axis), value.shape[dim])
        up = [(i, (i + 1) % size) for i in range(size if wrap else size - 1)]
        down = [(j, i) for i, j in up]
        last = lax.slice_in_dim(value, length - width, length, axis=dim)
        initial = lax.slice_in_dim(value, 0, width, axis=dim)
        before = lax.ppermute(last, axis, up)
        after = lax.ppermute(initial, axis, down)
        value = jnp.concatenate([before, value, after], axis=dim)
    return value


def body(
    test_field, dir_field, border_b, border_c, land_mask, active_rows, cell_blocks, column_k, kappa
):
    rows_here, units, layers, cells = test_field.shape
    col_size = column_k.shape[0]
    depth = col_size // units
    lines = jnp.arange(rows_here, dtype=jnp.int32)
    named = jnp.any(active_rows[:, 0][None, :] == lines[:, None], axis=1)
    weight = land_mask.astype(jnp.float32) * named.astype(jnp.float32)[:, None]
    stacked = jnp.concatenate(
        [
            test_field * weight.astype(jnp.bfloat16)[:, None, None, :],
            dir_field * weight.astype(jnp.bfloat16)[:, None, None, :],
        ],
        axis=1,
    )
    column_b = border_b.astype(jnp.float32)
    row_c = border_c.astype(jnp.float32)
    norm_b = jnp.sum(column_b * column_b)
    norm_c = jnp.sum(row_c * row_c)
    value_c = jnp.sum(row_c * test_field.astype(jnp.float32))
    part = lax.all_to_all(stacked, "lz", split_axis=0, concat_axis=2, tiled=True)
    group = part.shape[0]
    span = part.shape[3]
    flat = part.reshape(group, 2, col_size, span)
    product = jnp.einsum("pq,gfqc->gfpc", column_k, flat, preferred_element_type=jnp.float32)
    product = product.astype(jnp.bfloat16).reshape(group, 2 * units, depth, span)
    coupled = lax.all_to_all(product, "lz", split_axis=2, concat_axis=0, tiled=True).astype(
        jnp.float32
    )
    lon_padded = extended(stacked, (("tx", 0),), 1, True)
    lat_padded = extended(stacked, (("ty", 3),), 1, False)
    center = stacked.astype(jnp.float32)
    spread = (
        lon_padded[2:].astype(jnp.float32)
        + lon_padded[:-2].astype(jnp.float32)
        + lat_padded[..., 2:].astype(jnp.float32)
        + lat_padded[..., :-2].astype(jnp.float32)
        - 4.0 * center
    )
    rates = jnp.concatenate([kappa, kappa]).reshape(1, 2 * units, 1, 1)
    blocks = cell_blocks.reshape(rows_here, units, units, cells)
    local = jnp.einsum(
        "xuwy,xfwzy->xfuzy",
        blocks,
        stacked.reshape(rows_here, 2, units, layers, cells),
        preferred_element_type=jnp.float32,
    ).reshape(rows_here, 2 * units, layers, cells)
    image = weight[:, None, None, :] * (coupled + local + rates * spread)
    test_full = image[:, :units]
    dir_full = image[:, units:]
    value_a = jnp.sum(column_b * test_full)
    value_e = jnp.sum(column_b * dir_full)
    norm_b, norm_c, value_c, value_a, value_e = lax.psum(
        (norm_b, norm_c, value_c, value_a, value_e), ("tx", "ty", "lz")
    )
    border = jnp.stack(
        [value_a / jnp.sqrt(norm_b), value_e / jnp.sqrt(norm_b), value_c / jnp.sqrt(norm_c)]
    )
    return (test_full.astype(jnp.bfloat16), dir_full.astype(jnp.bfloat16), border)


def solution(mesh):
    in_specs = (
        P("tx", None, "lz", "ty"),
        P("tx", None, "lz", "ty"),
        P("tx", None, "lz", "ty"),
        P("tx", None, "lz", "ty"),
        P("tx", "ty"),
        P("tx", "ty"),
        P("tx", None, "ty"),
        P(),
        P(),
    )
    out_specs = (P("tx", None, "lz", "ty"), P("tx", None, "lz", "ty"), P())
    return jax.shard_map(body, mesh=mesh, in_specs=in_specs, out_specs=out_specs, check_vma=False)
```

profile of v0, /device:TPU:0, one launch (start us, length us, event | category | flops | bytes accessed | tf_op | source)
XLA Modules:
  0.0 150.9 jit_solution(9420423562500274029)
XLA Ops:
  0.6 0.0 copy-start
  0.6 0.8 fusion.13
  1.5 0.8 fusion.14
  2.3 1.3 broadcast_multiply_fusion.1
  3.6 0.1 pad_maximum_fusion
  3.7 1.7 %copy.43 = bf16[32,12,12,128]{3,2,1,0:T(8,128)(2,1)} copy(bf16[32,12,12,128]{3,0,2,1:T(8,128)(2,1)S(1)} %pad_maximum_fusion) | data formatting | bytes 2359296 | tf_op jit(solution)/shard_map/concatenate | solution.py:29
  5.4 6.3 %all-to-all-start = ((bf16[32,12,12,128]{3,2,1,0:T(8,128)(2,1)}), bf16[32,12,12,128]{3,2,1,0:T(8,128)(2,1)}, u32[]{:S(2)}, u32[]{:S(2)}) async-start(bf16[32,12,12,128]{3,2,1,0:T(8,128)(2,1)} %copy.43), calls=%async_computation | async-start | bytes 3145728 | tf_op jit(solution)/shard_map/all_to_all | solution.py:41
  11.7 1.9 %fusion.7 = (bf16[32,12,12,1]{3,0,2,1:T(8,128)(2,1)}, bf16[32,12,12,1]{3,0,2,1:T(8,128)(2,1)}) fusion(bf16[32,6,12,128]{3,0,2,1:T(8,128)(2,1)S(1)} %get-tuple-element.21, bf16[32,6,12,128]{3,0,2,1:T(8,128)(2,1)S(1)} %get-tuple-element.22), kind=kLoop, calls=%fused_computation.25 | loop fusion | flops 9216 | bytes 1198080 | tf_op jit(solution)/shard_map/concatenate | solution.py:29
  13.6 2.4 %copy.53 = bf16[32,12,12,1]{0,2,3,1:T(8,128)(2,1)S(1)} copy(bf16[32,12,12,1]{3,0,2,1:T(8,128)(2,1)} %get-tuple-element.19) | data formatting | bytes 18432 | tf_op jit(solution)/shard_map/slice | solution.py:13
  16.0 1.3 collective-permute-start.2
  17.3 2.5 %copy.55 = bf16[32,12,12,1]{0,2,3,1:T(8,128)(2,1)S(1)} copy(bf16[32,12,12,1]{3,0,2,1:T(8,128)(2,1)} %get-tuple-element.20) | data formatting | bytes 18432 | tf_op jit(solution)/shard_map/slice | solution.py:12
  19.8 4.6 %collective-permute-start.3 = (bf16[32,12,12,1]{0,2,3,1:T(8,128)(2,1)S(1)}, bf16[32,12,12,1]{0,2,3,1:T(8,128)(2,1)S(1)}, u32[]{:S(2)}, u32[]{:S(2)}) collective-permute-start(bf16[32,12,12,1]{0,2,3,1:T(8,128)(2,1)S(1)} %copy.55), channel_id=1, source_target_pairs={{0,4},{4,8},{8,12},{1,5},{5,9},{9,13},{2,6},{6,10},{10,14},{3,7},{... | collective-permute-start | bytes 27656 | tf_op jit(solution)/shard_map/ppermute | solution.py:14
  24.4 0.2 fusion.11
  24.5 0.1 collective-permute-start
  24.6 0.5 collective-permute-start.1
  25.1 10.2 %copy.50 = bf16[32,2,6,12,128]{3,2,1,4,0:T(8,128)(2,1)} copy(bf16[32,2,6,12,128]{4,0,3,2,1:T(8,128)(2,1)S(1)} %bitcast.37) | data formatting | bytes 2359296 | tf_op jit(solution)/shard_map/reshape | solution.py:65
  35.3 0.0 copy-done.6
  35.3 5.5 %copy.58 = bf16[32,6,6,128,1]{2,1,4,3,0:T(8,128)(2,1)} copy(bf16[32,6,6,128,1]{3,0,2,1,4:T(8,128)(2,1)S(1)} %bitcast.41) | data formatting | bytes 589824 | tf_op jit(solution)/shard_map/reshape | solution.py:61
  40.8 0.0 copy-done.3
  40.8 0.0 copy-done.4
  40.8 1.0 fusion.3
  41.8 7.0 %all-to-all-done = bf16[32,12,12,128]{3,2,1,0:T(8,128)(2,1)} async-done(((bf16[32,12,12,128]{3,2,1,0:T(8,128)(2,1)}), bf16[32,12,12,128]{3,2,1,0:T(8,128)(2,1)}, u32[]{:S(2)}, u32[]{:S(2)}) %all-to-all-start) | async-done | bytes 1179680 | tf_op jit(solution)/shard_map/all_to_all | solution.py:41
  48.8 2.8 %copy.45 = bf16[8,12,4,12,128]{4,0,3,2,1:T(8,128)(2,1)S(1)} copy(bf16[8,12,4,12,128]{4,3,1,0,2:T(8,128)(2,1)} %bitcast.3) | data formatting | bytes 2359296 | tf_op jit(solution)/shard_map/all_to_all | solution.py:41
  51.6 0.0 copy-done
  51.6 0.8 convolution_convert_fusion
  52.4 1.9 %copy.47 = bf16[8,12,48,128]{3,0,1,2:T(8,128)(2,1)} copy(bf16[8,12,48,128]{3,2,1,0:T(8,128)(2,1)S(1)} %bitcast.39) | data formatting | bytes 2359296 | tf_op jit(solution)/shard_map/reshape | solution.py:46
  54.2 4.5 %all-to-all-start.1 = ((bf16[8,12,48,128]{3,0,1,2:T(8,128)(2,1)}), bf16[8,12,48,128]{3,0,1,2:T(8,128)(2,1)}, u32[]{:S(2)}, u32[]{:S(2)}) async-start(bf16[8,12,48,128]{3,0,1,2:T(8,128)(2,1)} %copy.47), calls=%async_computation.1 | async-start | bytes 2359296 | tf_op jit(solution)/shard_map/all_to_all | solution.py:47
  58.7 0.0 copy-start.7
  58.7 20.0 %convolution_bitcast_fusion = f32[32,2,6,12,128]{3,2,1,4,0:T(8,128)} fusion(bf16[32,2,6,12,128]{3,2,1,4,0:T(8,128)(2,1)} %copy.50, bf16[32,6,6,128,1]{2,1,4,3,0:T(8,128)(2,1)} %copy.58), kind=kOutput, calls=%fused_computation | convolution fusion | flops 7077888 | bytes 3833856 | tf_op jit(solution)/shard_map/xuwy,xfwzy->xfuzy/dot_general | solution.py:62
  78.7 0.0 copy-done.7
  78.7 0.1 pad_maximum_fusion.9
  78.8 15.6 %copy.52 = f32[32,2,6,12,128]{4,0,3,2,1:T(8,128)} copy(f32[32,2,6,12,128]{3,2,1,4,0:T(8,128)} %convolution_bitcast_fusion) | data formatting | bytes 4718592 | tf_op jit(solution)/shard_map/xuwy,xfwzy->xfuzy/transpose | solution.py:62
  94.4 0.0 collective-permute-done.2
  94.4 1.0 copy.54
  95.4 0.0 collective-permute-done.3
  95.4 1.9 %copy.56 = bf16[32,12,12,1]{3,0,2,1:T(8,128)(2,1)} copy(bf16[32,12,12,1]{0,2,3,1:T(8,128)(2,1)S(1)} %collective-permute-done.3) | data formatting | bytes 18432 | tf_op jit(solution)/shard_map/ppermute | solution.py:14
  97.3 0.0 all-to-all-done.1
  97.3 1.6 %copy.48 = bf16[8,12,48,128]{3,0,2,1:T(8,128)(2,1)S(1)} copy(bf16[8,12,48,128]{3,0,1,2:T(8,128)(2,1)} %all-to-all-done.1) | data formatting | bytes 2359296 | tf_op jit(solution)/shard_map/all_to_all | solution.py:47
  99.0 0.0 collective-permute-done
  99.0 0.0 collective-permute-done.1
  99.0 0.0 copy-done.2
  99.0 4.8 %fusion.1 = f32[32,12,12,128]{3,0,2,1:T(8,128)S(1)} fusion(f32[32,2,6,12,128]{4,0,3,2,1:T(8,128)} %copy.52, bf16[32,12,12,1]{3,0,2,1:T(8,128)(2,1)S(1)} %copy-done.2, bf16[32,6,12,128]{3,0,2,1:T(8,128)(2,1)S(1)} %get-tuple-element.22, bf16[32,6,12,128]{3,0,2,1:T(8,128)(2,1)S(1)} %get-tuple-element.21, bf16[32,12,12,1]{3,0,2,1:T(8,128)(2,1)S(1)} %copy.54, ...), kind=kLoop, calls=%fused_computation.4 | loop fusion | flops 22413312 | bytes 7186480 | tf_op jit(solution)/shard_map/mul | solution.py:68
  103.8 0.0 copy-start.5
  103.8 0.0 copy-start.1
  103.8 1.3 fusion.15
  105.1 1.1 fusion.4
  106.2 40.9 %all-reduce = (f32[]{:T(128)}, f32[]{:T(128)}, f32[]{:T(128)}, f32[]{:T(128)}, f32[]{:T(128)}) all-reduce(f32[]{:T(128)} %get-tuple-element.7, f32[]{:T(128)} %get-tuple-element.6, f32[]{:T(128)} %get-tuple-element.4, f32[]{:T(128)} %get-tuple-element.5, f32[]{:T(128)} %get-tuple-element.3), channel_id=1, replica_groups=mesh['tx'=2,'ty'=4,'lz'=4] {'tx','ty','lz'}, use_global_device_ids=true, to_apply=%region_8.0 | all-reduce | flops 5 | bytes 40 | tf_op jit(solution)/shard_map/psum | solution.py:73
  150.3 0.6 pad_maximum_fusion.10
  (7 shorter events, 0.0 us)
Async XLA Ops:
  0.6 50.9 %copy-start = (bf16[288,288]{1,0:T(8,128)(2,1)S(1)}, bf16[288,288]{1,0:T(8,128)(2,1)}, u32[]{:S(2)}) copy-start(bf16[288,288]{1,0:T(8,128)(2,1)} %param.16) | copy-start | bytes 497668
  5.4 43.4 %all-to-all-start = ((bf16[32,12,12,128]{3,2,1,0:T(8,128)(2,1)}), bf16[32,12,12,128]{3,2,1,0:T(8,128)(2,1)}, u32[]{:S(2)}, u32[]{:S(2)}) async-start(bf16[32,12,12,128]{3,2,1,0:T(8,128)(2,1)} %copy.43), calls=%async_computation | async-start | bytes 3145728 | tf_op jit(solution)/shard_map/all_to_all | solution.py:41
  16.0 78.4 %collective-permute-start.2 = (bf16[32,12,12,1]{0,2,3,1:T(8,128)(2,1)S(1)}, bf16[32,12,12,1]{0,2,3,1:T(8,128)(2,1)S(1)}, u32[]{:S(2)}, u32[]{:S(2)}) collective-permute-start(bf16[32,12,12,1]{0,2,3,1:T(8,128)(2,1)S(1)} %copy.53), channel_id=1, source_target_pairs={{4,0},{8,4},{12,8},{5,1},{9,5},{13,9},{6,2},{10,6},{14,10},{7,3},{... | collective-permute-start | bytes 27656 | tf_op jit(solution)/shard_map/ppermute | solution.py:15
  19.8 75.6 %collective-permute-start.3 = (bf16[32,12,12,1]{0,2,3,1:T(8,128)(2,1)S(1)}, bf16[32,12,12,1]{0,2,3,1:T(8,128)(2,1)S(1)}, u32[]{:S(2)}, u32[]{:S(2)}) collective-permute-start(bf16[32,12,12,1]{0,2,3,1:T(8,128)(2,1)S(1)} %copy.55), channel_id=1, source_target_pairs={{0,4},{4,8},{8,12},{1,5},{5,9},{9,13},{2,6},{6,10},{10,14},{3,7},{... | collective-permute-start | bytes 27656 | tf_op jit(solution)/shard_map/ppermute | solution.py:14
  24.5 74.5 %collective-permute-start = (bf16[1,12,12,128]{3,0,2,1:T(2,128)(2,1)S(1)}, bf16[1,12,12,128]{3,0,2,1:T(2,128)(2,1)S(1)}, u32[]{:S(2)}, u32[]{:S(2)}) collective-permute-start(bf16[1,12,12,128]{3,0,2,1:T(2,128)(2,1)S(1)} %get-tuple-element.17), channel_id=1, source_target_pairs={{16,0},{0,16},{17,1},{1,17},{18,2},{2,18},{19,3},{3,19},{20,4},{4,... | collective-permute-start | bytes 110600 | tf_op jit(solution)/shard_map/ppermute | solution.py:15
  24.6 74.4 %collective-permute-start.1 = (bf16[1,12,12,128]{3,0,2,1:T(2,128)(2,1)S(1)}, bf16[1,12,12,128]{3,0,2,1:T(2,128)(2,1)S(1)}, u32[]{:S(2)}, u32[]{:S(2)}) collective-permute-start(bf16[1,12,12,128]{3,0,2,1:T(2,128)(2,1)S(1)} %get-tuple-element.18), channel_id=1, source_target_pairs={{0,16},{16,0},{1,17},{17,1},{2,18},{18,2},{3,19},{19,3},{4,20},{20... | collective-permute-start | bytes 110600 | tf_op jit(solution)/shard_map/ppermute | solution.py:14
  25.1 10.2 %copy-start.6 = (bf16[32,36,128]{2,0,1:T(8,128)(2,1)S(1)}, bf16[32,36,128]{2,0,1:T(8,128)(2,1)}, u32[]{:S(2)}) copy-start(bf16[32,36,128]{2,0,1:T(8,128)(2,1)} %param.15) | copy-start | bytes 884740
  35.3 5.5 %copy-start.3 = (bf16[32,6,12,128]{3,0,2,1:T(8,128)(2,1)S(1)}, bf16[32,6,12,128]{3,0,2,1:T(8,128)(2,1)}, u32[]{:S(2)}) copy-start(bf16[32,6,12,128]{3,0,2,1:T(8,128)(2,1)} %param.9) | copy-start | bytes 1769476
  35.3 5.5 %copy-start.4 = (bf16[32,6,12,128]{3,0,2,1:T(8,128)(2,1)S(1)}, bf16[32,6,12,128]{3,0,2,1:T(8,128)(2,1)}, u32[]{:S(2)}) copy-start(bf16[32,6,12,128]{3,0,2,1:T(8,128)(2,1)} %param.12) | copy-start | bytes 1769476
  54.2 43.1 %all-to-all-start.1 = ((bf16[8,12,48,128]{3,0,1,2:T(8,128)(2,1)}), bf16[8,12,48,128]{3,0,1,2:T(8,128)(2,1)}, u32[]{:S(2)}, u32[]{:S(2)}) async-start(bf16[8,12,48,128]{3,0,1,2:T(8,128)(2,1)} %copy.47), calls=%async_computation.1 | async-start | bytes 2359296 | tf_op jit(solution)/shard_map/all_to_all | solution.py:47
  58.7 20.0 %copy-start.7 = (f32[6]{0:T(128)S(1)}, f32[6]{0:T(128)}, u32[]{:S(2)}) copy-start(f32[6]{0:T(128)} %param.17) | copy-start | bytes 76
  97.3 1.7 %copy-start.2 = (bf16[32,12,12,1]{3,0,2,1:T(8,128)(2,1)S(1)}, bf16[32,12,12,1]{3,0,2,1:T(8,128)(2,1)}, u32[]{:S(2)}) copy-start(bf16[32,12,12,1]{3,0,2,1:T(8,128)(2,1)} %copy.56) | copy-start | bytes 27652
  103.8 1.3 copy-start.5
  103.8 47.1 %copy-start.1 = (bf16[288,288]{1,0:T(8,128)(2,1)S(1)}, bf16[288,288]{1,0:T(8,128)(2,1)}, u32[]{:S(2)}) copy-start(bf16[288,288]{1,0:T(8,128)(2,1)} %param.16) | copy-start | bytes 497668
where the time goes:
time: 152 us; the launch traced here: 151 us
  local copies, waits for them, and re-layouts  48.4 us (32%)
  blocking collectives  40.9 us (27%)
  matrix products  20.8 us (14%)
  starting transfers between devices  17.2 us (11%)
  other arithmetic  12.6 us (8%)
  waiting for transfers between devices  7.02 us (5%)
  between operations  3.94 us (3%)
    psum x1, blocking collectives, body(): lax.psum((norm_b, norm_c, value_c, value_a, value_e), ('tx', 'ty', 'lz'))  40.9 us
    dot_general x1, matrix products, body(): jnp.einsum('xuwy,xfwzy->xfuzy', blocks, stacked.reshape(rows_here, 2, uni...  20 us
    transpose x1, local copies, waits for them, and re-layouts, body(): jnp.einsum('xuwy,xfwzy->xfuzy', blocks, stacked.reshape(rows_here, 2, uni...  15.6 us
    reshape x1, local copies, waits for them, and re-layouts, body(): stacked.reshape(rows_here, 2, units, layers, cells)  10.2 us
    all_to_all x1, waiting for transfers between devices, body(): lax.all_to_all(stacked, 'lz', split_axis=0, concat_axis=2, tiled=True)  7.01 us
    all_to_all x1, starting transfers between devices, body(): lax.all_to_all(stacked, 'lz', split_axis=0, concat_axis=2, tiled=True)  6.35 us
    reshape x1, local copies, waits for them, and re-layouts, body(): blocks = cell_blocks.reshape(rows_here, units, units, cells)  5.47 us
    ppermute x2, starting transfers between devices, extended(): before = lax.ppermute(last, axis, up)  5.05 us
  transfers between devices with their start and end apart: 6, of which 1 were waited for; matrix products, arithmetic and copies ran while one was open for 46% of the time, Pallas kernels for 0%

commit v1 on v0

v1 whole, which is shorter than its diff:
```python
import functools
import jax
import jax.numpy as jnp
from jax import lax
from jax.experimental import pallas as pl
from jax.experimental.pallas import tpu as pltpu
from jax.sharding import PartitionSpec as P

MESH = pl.DeviceIdType.MESH
F32 = jnp.float32
BF16 = jnp.bfloat16


def kernel(
    sizes, chunks,
    test_ref, dir_ref, b_ref, c_ref, land_ref, active_ref, blocks_ref, k_ref, kappa_ref,
    out_t, out_d, border_ref,
    masked, arrived, product, coupled, weight, rates, big_k, pack, spread_s, blocks_s,
    edge_out, edge_in, edge_f, stat_out, stat_z, stat_y, stat_x,
    fs, fr, bs, br, xs, xr, ys, yr, ss, sr_z, sr_y, sr_x,
):
    nx, ny, nz = sizes
    rows, units, layers, cells = test_ref.shape
    slab = units * layers
    full = 2 * slab
    group = rows // nz
    step = group // chunks
    mx, my, mz = lax.axis_index("tx"), lax.axis_index("ty"), lax.axis_index("lz")
    fields = (test_ref, dir_ref)

    barrier = pltpu.get_barrier_semaphore()
    for name, me, size in (("tx", mx, nx), ("ty", my, ny), ("lz", mz, nz)):
        for k in range(1, size):
            pl.semaphore_signal(
                barrier, inc=1, device_id={name: lax.rem(me + k, size)}, device_id_type=MESH
            )

    lane = lax.broadcasted_iota(jnp.int32, (full, cells), 1)
    active = jnp.broadcast_to(active_ref[...], (rows, cells))

    def pack_row(x, edges):
        named = jnp.max((active == x).astype(F32), axis=0, keepdims=True)
        row = land_ref[pl.ds(x, 1), :].astype(F32) * named
        weight[pl.ds(x, 1), :] = row
        for f in range(2):
            for u in range(units):
                value = fields[f][x, u].astype(F32) * row
                pack[pl.ds(f * slab + u * layers, layers), :] = value
        value = pack[...]
        masked[x + 1] = value.astype(BF16)
        first = pltpu.roll(value, x, 1)
        last = pltpu.roll(value, lax.rem(rows + x + 1, cells), 1)
        edges = jnp.where(lane == x, first, edges)
        return jnp.where(lane == rows + x, last, edges)

    edges = lax.fori_loop(0, rows, pack_row, jnp.zeros((full, cells), F32))
    edge_out[...] = edges.astype(BF16)

    def own_row(i, carry):
        arrived[lax.div(i, step), mz, lax.rem(i, step)] = masked[1 + mz * group + i]
        return carry

    lax.fori_loop(0, group, own_row, 0)

    pl.semaphore_wait(barrier, (nx - 1) + (ny - 1) + (nz - 1))

    def forward(c, k):
        to = lax.rem(mz + k, nz)
        return pltpu.make_async_remote_copy(
            src_ref=masked.at[pl.ds(1 + to * group + c * step, step)],
            dst_ref=arrived.at[c, mz],
            send_sem=fs.at[c, to],
            recv_sem=fr.at[c, mz],
            device_id={"lz": to},
            device_id_type=MESH,
        )

    def forward_in(c, k):
        src = lax.rem(mz + nz - k, nz)
        return pltpu.make_async_remote_copy(
            src_ref=arrived.at[c, src],
            dst_ref=arrived.at[c, src],
            send_sem=fs.at[c, src],
            recv_sem=fr.at[c, src],
            device_id={"lz": src},
            device_id_type=MESH,
        )

    def backward(c, k):
        to = lax.rem(mz + k, nz)
        return pltpu.make_async_remote_copy(
            src_ref=product.at[c, to],
            dst_ref=coupled.at[pl.ds(mz * group + c * step, step)],
            send_sem=bs.at[c, to],
            recv_sem=br.at[c, mz],
            device_id={"lz": to},
            device_id_type=MESH,
        )

    def backward_in(c, k):
        src = lax.rem(mz + nz - k, nz)
        return pltpu.make_async_remote_copy(
            src_ref=product.at[c, src],
            dst_ref=coupled.at[pl.ds(src * group + c * step, step)],
            send_sem=bs.at[c, src],
            recv_sem=br.at[c, src],
            device_id={"lz": src},
            device_id_type=MESH,
        )

    order = sorted(range(1, nz), key=lambda k: -min(k, nz - k))
    for k in order:
        forward(0, k).start()
    later, before = lax.rem(mx + 1, nx), lax.rem(mx + nx - 1, nx)
    to_later = pltpu.make_async_remote_copy(
        src_ref=masked.at[rows], dst_ref=masked.at[0], send_sem=xs.at[0], recv_sem=xr.at[0],
        device_id={"tx": later}, device_id_type=MESH,
    )
    to_before = pltpu.make_async_remote_copy(
        src_ref=masked.at[1], dst_ref=masked.at[rows + 1], send_sem=xs.at[1], recv_sem=xr.at[1],
        device_id={"tx": before}, device_id_type=MESH,
    )
    to_later.start()
    to_before.start()
    up, down = lax.rem(my + 1, ny), lax.rem(my + ny - 1, ny)
    to_up = pltpu.make_async_remote_copy(
        src_ref=edge_out, dst_ref=edge_in.at[0], send_sem=ys.at[0], recv_sem=yr.at[0],
        device_id={"ty": up}, device_id_type=MESH,
    )
    to_down = pltpu.make_async_remote_copy(
        src_ref=edge_out, dst_ref=edge_in.at[1], send_sem=ys.at[1], recv_sem=yr.at[1],
        device_id={"ty": down}, device_id_type=MESH,
    )
    to_up.start()
    to_down.start()
    for c in range(1, chunks):
        for k in order:
            forward(c, k).start()

    for f in range(2):
        for u in range(units):
            rates[pl.ds(f * slab + u * layers, layers), :] = jnp.full(
                (layers, cells), kappa_ref[u], F32
            )

    col = units * layers * nz
    wide = nz * full

    def chooser(shape, dim, f):
        i = lax.broadcasted_iota(jnp.int32, shape, dim)
        j = lax.broadcasted_iota(jnp.int32, shape, 1 - dim)
        part, rest = i // full, lax.rem(i, full)
        field, entry = rest // slab, lax.rem(rest, slab)
        unit, layer = entry // layers, lax.rem(entry, layers)
        target = unit * (layers * nz) + part * layers + layer
        return jnp.where((target == j) & (field == f), 1.0, 0.0).astype(BF16)

    dense = k_ref[...]
    total = None
    for f in range(2):
        left = jnp.dot(
            chooser((wide, col), 0, f), dense, preferred_element_type=F32
        ).astype(BF16)
        both = jnp.dot(left, chooser((col, wide), 1, f), preferred_element_type=F32)
        total = both if total is None else total + both
    big_k[...] = total.astype(BF16)

    zero = jnp.zeros((layers, cells), F32)
    sums = (zero, zero, zero)

    def norms(x, carry):
        bb, cc, cv = carry
        for u in range(units):
            b = b_ref[x, u].astype(F32)
            c = c_ref[x, u].astype(F32)
            bb = bb + b * b
            cc = cc + c * c
            cv = cv + c * test_ref[x, u].astype(F32)
        return bb, cc, cv

    quarter = rows // chunks
    for c in range(chunks):
        for k in order:
            forward_in(c, k).wait_recv()
        part = jnp.concatenate(
            [arrived[c, :, r].reshape(wide, cells) for r in range(step)], axis=1
        )
        result = jnp.dot(big_k[...], part, preferred_element_type=F32).astype(BF16)
        for d in range(nz):
            for r in range(step):
                product[c, d, r] = result[d * full:(d + 1) * full, r * cells:(r + 1) * cells]
        sums = lax.fori_loop(c * quarter, (c + 1) * quarter, norms, sums)
        for k in order:
            backward(c, k).start()
        for r in range(step):
            coupled[mz * group + c * step + r] = product[c, mz, r]

    to_later.wait_recv()
    to_before.wait_recv()
    to_up.wait_recv()
    to_down.wait_recv()

    @pl.when(my > 0)
    def _():
        edge_f[0] = edge_in[0].astype(F32)

    @pl.when(my == 0)
    def _():
        edge_f[0] = jnp.zeros((full, cells), F32)

    @pl.when(my < ny - 1)
    def _():
        edge_f[1] = edge_in[1].astype(F32)

    @pl.when(my == ny - 1)
    def _():
        edge_f[1] = jnp.zeros((full, cells), F32)

    def image_row(x, carry):
        ba, be = carry
        here = masked[x + 1].astype(F32)
        south = jnp.where(
            lane == 0, pltpu.roll(edge_f[0], lax.rem(2 * cells - rows - x, cells), 1),
            pltpu.roll(here, 1, 1),
        )
        north = jnp.where(
            lane == cells - 1, pltpu.roll(edge_f[1], cells - 1 - x, 1),
            pltpu.roll(here, cells - 1, 1),
        )
        near = masked[x].astype(F32) + masked[x + 2].astype(F32) + south + north - 4.0 * here
        spread_s[...] = coupled[x].astype(F32) + rates[...] * near
        blocks_s[...] = blocks_ref[x].astype(F32)
        row = weight[pl.ds(x, 1), :]
        source = [[fields[f][x, w].astype(F32) * row for w in range(units)] for f in range(2)]
        for u in range(units):
            mix = [blocks_s[pl.ds(units * u + w, 1), :] for w in range(units)]
            b = b_ref[x, u].astype(F32)
            images = []
            for f in range(2):
                value = spread_s[pl.ds(f * slab + u * layers, layers), :]
                for w in range(units):
                    value = value + mix[w] * source[f][w]
                images.append(row * value)
            out_t[x, u] = images[0].astype(BF16)
            out_d[x, u] = images[1].astype(BF16)
            ba = ba + b * images[0]
            be = be + b * images[1]
        return ba, be

    pair = (zero, zero)
    for c in range(chunks):
        for k in order:
            backward_in(c, k).wait_recv()

        def chunk_row(i, carry):
            x = lax.div(i, step) * group + c * step + lax.rem(i, step)
            return image_row(x, carry)

        pair = lax.fori_loop(0, nz * step, chunk_row, pair)

    lines = [jnp.sum(v, axis=0, keepdims=True) for v in (*sums, *pair)]
    value = jnp.concatenate(lines + [jnp.zeros((3, cells), F32)], axis=0)
    base = 0
    stages = (
        ("lz", mz, nz, stat_z, sr_z), ("ty", my, ny, stat_y, sr_y), ("tx", mx, nx, stat_x, sr_x)
    )
    sends = []
    for s, (name, me, size, box, sem) in enumerate(stages):
        stat_out[s] = value
        box[me] = value
        for k in range(1, size):
            copy = pltpu.make_async_remote_copy(
                src_ref=stat_out.at[s], dst_ref=box.at[me], send_sem=ss.at[base + k - 1],
                recv_sem=sem.at[me], device_id={name: lax.rem(me + k, size)},
                device_id_type=MESH,
            )
            copy.start()
            sends.append(copy)
        base += size - 1
        for k in range(1, size):
            src = lax.rem(me + size - k, size)
            pltpu.make_async_remote_copy(
                src_ref=stat_out.at[s], dst_ref=box.at[src], send_sem=ss.at[0],
                recv_sem=sem.at[src], device_id={name: src}, device_id_type=MESH,
            ).wait_recv()
        value = box[0]
        for i in range(1, size):
            value = value + box[i]
    final = jnp.broadcast_to(jnp.sum(value, axis=1, keepdims=True), (8, cells))
    bb, cc, cv, ba, be = (final[i:i + 1] for i in range(5))
    line = lax.broadcasted_iota(jnp.int32, (1, cells), 1)
    top = jnp.where(line == 0, ba, jnp.where(line == 1, be, cv))
    low = jnp.where(line == 2, cc, bb)
    border_ref[...] = top / jnp.sqrt(low)

    for c in range(chunks):
        for k in order:
            forward(c, k).wait_send()
            backward(c, k).wait_send()
    to_later.wait_send()
    to_before.wait_send()
    to_up.wait_send()
    to_down.wait_send()
    for copy in sends:
        copy.wait_send()


def body(sizes, *arrays):
    test_field = arrays[0]
    nx, ny, nz = sizes
    rows, units, layers, cells = test_field.shape
    full = 2 * units * layers
    group = rows // nz
    chunks = 4 if group % 4 == 0 else 1
    step = group // chunks
    mixes = arrays[6].shape[1]
    vmem = pl.BlockSpec(memory_space=pltpu.VMEM)
    smem = pl.BlockSpec(memory_space=pltpu.SMEM)
    dma = pltpu.SemaphoreType.DMA
    out_t, out_d, border = pl.pallas_call(
        functools.partial(kernel, sizes, chunks),
        out_shape=(
            jax.ShapeDtypeStruct(test_field.shape, BF16),
            jax.ShapeDtypeStruct(test_field.shape, BF16),
            jax.ShapeDtypeStruct((1, cells), F32),
        ),
        in_specs=[vmem] * 8 + [smem],
        out_specs=(vmem, vmem, vmem),
        scratch_shapes=[
            pltpu.VMEM((rows + 2, full, cells), BF16),
            pltpu.VMEM((chunks, nz, step, full, cells), BF16),
            pltpu.VMEM((chunks, nz, step, full, cells), BF16),
            pltpu.VMEM((rows, full, cells), BF16),
            pltpu.VMEM((rows, cells), F32),
            pltpu.VMEM((full, cells), F32),
            pltpu.VMEM((nz * full, nz * full), BF16),
            pltpu.VMEM((full, cells), F32),
            pltpu.VMEM((full, cells), F32),
            pltpu.VMEM((mixes, cells), F32),
            pltpu.VMEM((full, cells), BF16),
            pltpu.VMEM((2, full, cells), BF16),
            pltpu.VMEM((2, full, cells), F32),
            pltpu.VMEM((3, 8, cells), F32),
            pltpu.VMEM((nz, 8, cells), F32),
            pltpu.VMEM((ny, 8, cells), F32),
            pltpu.VMEM((nx, 8, cells), F32),
            dma((chunks, nz)),
            dma((chunks, nz)),
            dma((chunks, nz)),
            dma((chunks, nz)),
            dma((2,)),
            dma((2,)),
            dma((2,)),
            dma((2,)),
            dma((nx + ny + nz - 3,)),
            dma((nz,)),
            dma((ny,)),
            dma((nx,)),
        ],
        compiler_params=pltpu.CompilerParams(
            collective_id=0, has_side_effects=True, vmem_limit_bytes=48 * 1024 * 1024
        ),
    )(*arrays)
    return out_t, out_d, border[0, :3]


def solution(mesh):
    wide = P("tx", None, "lz", "ty")
    in_specs = (
        wide, wide, wide, wide, P("tx", "ty"), P("tx", "ty"), P("tx", None, "ty"), P(), P(),
    )
    sizes = tuple(mesh.shape[name] for name in ("tx", "ty", "lz"))
    return jax.shard_map(
        functools.partial(body, sizes), mesh=mesh, in_specs=in_specs,
        out_specs=(wide, wide, P()), check_vma=False,
    )
```

time: 152 us -> 79 us (0.52)
  Pallas kernels: 0 us -> 69.4 us
  blocking collectives: 40.9 us -> 0 us
  local copies, waits for them, and re-layouts: 48.4 us -> 8.59 us
  matrix products: 20.8 us -> 0 us
  starting transfers between devices: 17.2 us -> 0 us
  other arithmetic: 12.6 us -> 0 us
  waiting for transfers between devices: 7.02 us -> 0 us
  between operations: 3.94 us -> 0.69 us
    pallas_call x0 -> x1, Pallas kernels: none -> 69.4 us  [body(): pl.pallas_call(functools.partial(kernel, sizes, chunks), out_shape=(jax.S...]
    psum x1 -> x0, blocking collectives: 40.9 us -> none  [body(): lax.psum((norm_b, norm_c, value_c, value_a, value_e), ('tx', 'ty', 'lz'))]
    dot_general x2 -> x0, matrix products: 20.8 us -> none  [the longest x1 20 us: body(): jnp.einsum('xuwy,xfwzy->xfuzy', blocks, stacked.reshape(rows_here, 2, uni...]
    reshape x3 -> x0, local copies, waits for them, and re-layouts: 17.5 us -> none  [the longest x1 10.2 us: body(): stacked.reshape(rows_here, 2, units, layers, cells)]
    transpose x1 -> x0, local copies, waits for them, and re-layouts: 15.6 us -> none  [body(): jnp.einsum('xuwy,xfwzy->xfuzy', blocks, stacked.reshape(rows_here, 2, uni...]
    all_to_all x2 -> x0, starting transfers between devices: 10.8 us -> none  [the longest x1 6.35 us: body(): lax.all_to_all(stacked, 'lz', split_axis=0, concat_axis=2, tiled=True)]
    unnamed x16 -> x22, local copies, waits for them, and re-layouts: 0.05 us -> 8.08 us
    all_to_all x2 -> x0, waiting for transfers between devices: 7.01 us -> none  [the longest x1 7.01 us: body(): lax.all_to_all(stacked, 'lz', split_axis=0, concat_axis=2, tiled=True)]
  transfers between devices with their start and end apart: 6 -> 0, of which waited for: 1 -> 0; matrix products, arithmetic and copies ran while one was open for 46% -> 0% of each run, Pallas kernels for 0% -> 0%
where the time goes in v1:
time: 79 us; the launch traced here: 78.7 us
  Pallas kernels  69.4 us (88%)
  local copies, waits for them, and re-layouts  8.59 us (11%)
    pallas_call x1, Pallas kernels, body(): pl.pallas_call(functools.partial(kernel, sizes, chunks), out_shape=(jax.S...  69.4 us
    unnamed x22, local copies, waits for them, and re-layouts  8.08 us

profile of v1, /device:TPU:0, one launch (start us, length us, event | category | flops | bytes accessed | tf_op | source)
XLA Modules:
  0.0 78.7 jit_solution(8366682262179788378)
XLA Ops:
  0.6 0.0 copy-start.3
  0.6 0.8 %copy.16.active_ref = s32[32,1]{1,0:T(8,128)S(1)} copy(s32[32,1]{0,1:T(1,128)} %param.14) | data formatting | bytes 256 | tf_op args[5]
  1.4 1.1 %copy.17.blocks_ref = bf16[32,36,128]{2,1,0:T(8,128)(2,1)S(1)} copy(bf16[32,36,128]{2,0,1:T(8,128)(2,1)} %param.15) | data formatting | bytes 589824 | tf_op args[6]
  2.5 0.0 copy-done.3
  2.5 0.0 copy-start.4
  2.5 0.3 copy.12.test_ref
  2.8 0.8 %copy-done.4 = bf16[32,6,12,128]{3,0,2,1:T(8,128)(2,1)S(1)} copy-done((bf16[32,6,12,128]{3,0,2,1:T(8,128)(2,1)S(1)}, bf16[32,6,12,128]{3,0,2,1:T(8,128)(2,1)}, u32[]{:S(2)}) %copy-start.4) | copy-done | bytes 589848
  3.6 0.0 copy-start.5
  3.6 0.3 copy.13.dir_ref
  3.9 0.8 %copy-done.5 = bf16[32,6,12,128]{3,0,2,1:T(8,128)(2,1)S(1)} copy-done((bf16[32,6,12,128]{3,0,2,1:T(8,128)(2,1)S(1)}, bf16[32,6,12,128]{3,0,2,1:T(8,128)(2,1)}, u32[]{:S(2)}) %copy-start.5) | copy-done | bytes 589848
  4.7 0.0 copy-start.6
  4.7 0.3 copy.14.b_ref
  4.9 0.8 %copy-done.6 = bf16[32,6,12,128]{3,0,2,1:T(8,128)(2,1)S(1)} copy-done((bf16[32,6,12,128]{3,0,2,1:T(8,128)(2,1)S(1)}, bf16[32,6,12,128]{3,0,2,1:T(8,128)(2,1)}, u32[]{:S(2)}) %copy-start.6) | copy-done | bytes 589848
  5.7 0.0 copy-start
  5.7 0.0 copy-start.1
  5.7 0.0 copy-start.2
  5.7 0.3 copy.15.c_ref
  6.0 0.7 copy-done
  6.7 0.0 copy-done.1
  6.7 0.0 copy-done.2
  6.7 69.4 %shard_map.112 = (bf16[32,6,12,128]{3,2,1,0:T(8,128)(2,1)S(1)}, bf16[32,6,12,128]{3,2,1,0:T(8,128)(2,1)S(1)}, f32[1,128]{1,0:T(1,128)S(1)}) custom-call(bf16[32,6,12,128]{3,2,1,0:T(8,128)(2,1)S(1)} %copy.12.test_ref, bf16[32,6,12,128]{3,2,1,0:T(8,128)(2,1)S(1)} %copy.13.dir_ref, bf16[32,6,12,128]{3,2,1,0:T(8,128)(2,1)S(1)} %copy.14.b_ref, ...), custom_call_target="tpu_custom_call" | custom-call | tf_op jit(solution)/shard_map/pallas_call | solution.py:320
  76.1 1.0 %copy.18 = bf16[32,6,12,128]{3,0,2,1:T(8,128)(2,1)} copy(bf16[32,6,12,128]{3,2,1,0:T(8,128)(2,1)S(1)} %get-tuple-element.9) | data formatting | bytes 1179648
  77.1 0.5 slice_bitcast_fusion
  77.6 1.0 %copy.19 = bf16[32,6,12,128]{3,0,2,1:T(8,128)(2,1)} copy(bf16[32,6,12,128]{3,2,1,0:T(8,128)(2,1)S(1)} %get-tuple-element.10) | data formatting | bytes 1179648
Async XLA Ops:
  0.6 1.9 %copy-start.3 = (bf16[32,6,12,128]{3,0,2,1:T(8,128)(2,1)S(1)}, bf16[32,6,12,128]{3,0,2,1:T(8,128)(2,1)}, u32[]{:S(2)}) copy-start(bf16[32,6,12,128]{3,0,2,1:T(8,128)(2,1)} %param.9) | copy-start | bytes 1769476
  2.5 1.1 %copy-start.4 = (bf16[32,6,12,128]{3,0,2,1:T(8,128)(2,1)S(1)}, bf16[32,6,12,128]{3,0,2,1:T(8,128)(2,1)}, u32[]{:S(2)}) copy-start(bf16[32,6,12,128]{3,0,2,1:T(8,128)(2,1)} %param.10) | copy-start | bytes 1769476
  3.6 1.1 %copy-start.5 = (bf16[32,6,12,128]{3,0,2,1:T(8,128)(2,1)S(1)}, bf16[32,6,12,128]{3,0,2,1:T(8,128)(2,1)}, u32[]{:S(2)}) copy-start(bf16[32,6,12,128]{3,0,2,1:T(8,128)(2,1)} %param.11) | copy-start | bytes 1769476
  4.7 1.1 %copy-start.6 = (bf16[32,6,12,128]{3,0,2,1:T(8,128)(2,1)S(1)}, bf16[32,6,12,128]{3,0,2,1:T(8,128)(2,1)}, u32[]{:S(2)}) copy-start(bf16[32,6,12,128]{3,0,2,1:T(8,128)(2,1)} %param.12) | copy-start | bytes 1769476
  5.7 0.9 %copy-start = (bf16[288,288]{1,0:T(8,128)(2,1)S(1)}, bf16[288,288]{1,0:T(8,128)(2,1)}, u32[]{:S(2)}) copy-start(bf16[288,288]{1,0:T(8,128)(2,1)} %k_ref.1) | copy-start | bytes 497668
  5.7 0.9 %copy-start.1 = (s32[32,128]{1,0:T(8,128)S(1)}, s32[32,128]{1,0:T(8,128)}, u32[]{:S(2)}) copy-start(s32[32,128]{1,0:T(8,128)} %land_ref.1) | copy-start | bytes 49156
  5.7 0.9 %copy-start.2 = (f32[6]{0:T(128)S(1)}, f32[6]{0:T(128)}, u32[]{:S(2)}) copy-start(f32[6]{0:T(128)} %kappa_ref.1) | copy-start | bytes 76

commit v2 on v1

v2 whole, which is shorter than its diff:
```python
import functools
import jax
import jax.numpy as jnp
from jax import lax
from jax.experimental import pallas as pl
from jax.experimental.pallas import tpu as pltpu
from jax.sharding import PartitionSpec as P

MESH = pl.DeviceIdType.MESH
F32 = jnp.float32
BF16 = jnp.bfloat16


MARGIN = 8


def kernel(
    sizes, chunks, units,
    test_hbm, dir_hbm, b_hbm, c_hbm, land_ref, active_ref, blocks_hbm, k_hbm, kappa_ref,
    out_t, out_d, border_ref,
    test_ref, dir_ref, b_ref, c_ref, blocks_ref, k_ref,
    masked, arrived, product, coupled, weight, big_k, field, back, before_image, halo,
    edge_out, edge_in, edge_f, stat_out, stat_z, stat_y, stat_x,
    ls, fs, fr, bs, br, xs, xr, ys, yr, ss, sr_z, sr_y, sr_x,
):
    nx, ny, nz = sizes
    slab, rows, cells = test_ref.shape
    layers = slab // units
    full = 2 * slab
    group = rows // nz
    step = group // chunks
    pitch = rows + 2 * MARGIN
    mx, my, mz = lax.axis_index("tx"), lax.axis_index("ty"), lax.axis_index("lz")
    fields = (test_ref, dir_ref)
    outs = (out_t, out_d)

    loads = [
        pltpu.make_async_copy(source, target, ls.at[i])
        for i, (source, target) in enumerate((
            (test_hbm, test_ref), (dir_hbm, dir_ref), (k_hbm, k_ref), (b_hbm, b_ref),
            (c_hbm, c_ref), (blocks_hbm, blocks_ref),
        ))
    ]
    for load in loads:
        load.start()

    barrier = pltpu.get_barrier_semaphore()
    for name, me, size in (("tx", mx, nx), ("ty", my, ny), ("lz", mz, nz)):
        for k in range(1, size):
            pl.semaphore_signal(
                barrier, inc=1, device_id={name: lax.rem(me + k, size)}, device_id_type=MESH
            )

    lane = lax.broadcasted_iota(jnp.int32, (rows, cells), 1)
    line = lax.broadcasted_iota(jnp.int32, (rows, rows), 0)
    named = jnp.max(
        jnp.where(jnp.broadcast_to(active_ref[...], (rows, rows)) == line, 1.0, 0.0),
        axis=1, keepdims=True,
    )
    weight[...] = land_ref[...].astype(F32) * named
    ocean = weight[...]

    def middle(q):
        return pl.ds(pl.multiple_of(q * pitch + MARGIN, 8), rows)

    for f in range(2):
        loads[f].wait()

        def mask(j, edges):
            first, last = edges
            value = fields[f][j].astype(F32) * ocean
            field[middle(f * slab + j), :] = value
            first = jnp.where(lane == j, pltpu.roll(value, j, 1), first)
            last = jnp.where(lane == j, pltpu.roll(value, j + 1, 1), last)
            return first, last

        blank = jnp.zeros((rows, cells), F32)
        first, last = lax.fori_loop(0, slab, mask, (blank, blank), unroll=2)
        edge_out[0, f] = first.astype(BF16)
        edge_out[1, f] = last.astype(BF16)

    def pack(x, carry):
        masked[x] = field[pl.ds(MARGIN + x, full, stride=pitch), :].astype(BF16)
        return carry

    lax.fori_loop(0, rows, pack, 0, unroll=2)

    def own_row(i, carry):
        arrived[lax.div(i, step), mz, lax.rem(i, step)] = masked[mz * group + i]
        return carry

    lax.fori_loop(0, group, own_row, 0)

    pl.semaphore_wait(barrier, (nx - 1) + (ny - 1) + (nz - 1))

    def forward(c, k):
        to = lax.rem(mz + k, nz)
        return pltpu.make_async_remote_copy(
            src_ref=masked.at[pl.ds(to * group + c * step, step)],
            dst_ref=arrived.at[c, mz],
            send_sem=fs.at[c, to],
            recv_sem=fr.at[c, mz],
            device_id={"lz": to},
            device_id_type=MESH,
        )

    def forward_in(c, k):
        src = lax.rem(mz + nz - k, nz)
        return pltpu.make_async_remote_copy(
            src_ref=arrived.at[c, src],
            dst_ref=arrived.at[c, src],
            send_sem=fs.at[c, src],
            recv_sem=fr.at[c, src],
            device_id={"lz": src},
            device_id_type=MESH,
        )

    def backward(c, k):
        to = lax.rem(mz + k, nz)
        return pltpu.make_async_remote_copy(
            src_ref=product.at[c, to],
            dst_ref=coupled.at[pl.ds(mz * group + c * step, step)],
            send_sem=bs.at[c, to],
            recv_sem=br.at[c, mz],
            device_id={"lz": to},
            device_id_type=MESH,
        )

    def backward_in(c, k):
        src = lax.rem(mz + nz - k, nz)
        return pltpu.make_async_remote_copy(
            src_ref=product.at[c, src],
            dst_ref=coupled.at[pl.ds(src * group + c * step, step)],
            send_sem=bs.at[c, src],
            recv_sem=br.at[c, src],
            device_id={"lz": src},
            device_id_type=MESH,
        )

    order = sorted(range(1, nz), key=lambda k: -min(k, nz - k))
    for k in order:
        forward(0, k).start()
    later, before = lax.rem(mx + 1, nx), lax.rem(mx + nx - 1, nx)
    to_later = pltpu.make_async_remote_copy(
        src_ref=masked.at[rows - 1], dst_ref=halo.at[0], send_sem=xs.at[0], recv_sem=xr.at[0],
        device_id={"tx": later}, device_id_type=MESH,
    )
    to_before = pltpu.make_async_remote_copy(
        src_ref=masked.at[0], dst_ref=halo.at[1], send_sem=xs.at[1], recv_sem=xr.at[1],
        device_id={"tx": before}, device_id_type=MESH,
    )
    to_later.start()
    to_before.start()
    up, down = lax.rem(my + 1, ny), lax.rem(my + ny - 1, ny)
    to_up = pltpu.make_async_remote_copy(
        src_ref=edge_out.at[1], dst_ref=edge_in.at[0], send_sem=ys.at[0], recv_sem=yr.at[0],
        device_id={"ty": up}, device_id_type=MESH,
    )
    to_down = pltpu.make_async_remote_copy(
        src_ref=edge_out.at[0], dst_ref=edge_in.at[1], send_sem=ys.at[1], recv_sem=yr.at[1],
        device_id={"ty": down}, device_id_type=MESH,
    )
    to_up.start()
    to_down.start()
    for c in range(1, chunks):
        for k in order:
            forward(c, k).start()

    col = units * layers * nz
    wide = nz * full

    def chooser(shape, dim, f):
        i = lax.broadcasted_iota(jnp.int32, shape, dim)
        j = lax.broadcasted_iota(jnp.int32, shape, 1 - dim)
        part, rest = i // full, lax.rem(i, full)
        field, entry = rest // slab, lax.rem(rest, slab)
        unit, layer = entry // layers, lax.rem(entry, layers)
        target = unit * (layers * nz) + part * layers + layer
        return jnp.where((target == j) & (field == f), 1.0, 0.0).astype(BF16)

    loads[2].wait()
    dense = k_ref[...]
    total = None
    for f in range(2):
        left = jnp.dot(
            chooser((wide, col), 0, f), dense, preferred_element_type=F32
        ).astype(BF16)
        both = jnp.dot(left, chooser((col, wide), 1, f), preferred_element_type=F32)
        total = both if total is None else total + both
    big_k[...] = total.astype(BF16)

    for load in loads[3:]:
        load.wait()
    zero = jnp.zeros((rows, cells), F32)
    sums = (zero, zero, zero)

    def norms(j, carry):
        bb, cc, cv = carry
        b = b_ref[j].astype(F32)
        c = c_ref[j].astype(F32)
        return bb + b * b, cc + c * c, cv + c * test_ref[j].astype(F32)

    quarter = slab // chunks
    for c in range(chunks):
        for k in order:
            forward_in(c, k).wait_recv()
        part = jnp.concatenate(
            [arrived[c, :, r].reshape(wide, cells) for r in range(step)], axis=1
        )
        result = jnp.dot(big_k[...], part, preferred_element_type=F32).astype(BF16)
        for d in range(nz):
            for r in range(step):
                product[c, d, r] = result[d * full:(d + 1) * full, r * cells:(r + 1) * cells]
        sums = lax.fori_loop(c * quarter, (c + 1) * quarter, norms, sums)
        for k in order:
            backward(c, k).start()
        for r in range(step):
            coupled[mz * group + c * step + r] = product[c, mz, r]

    to_later.wait_recv()
    to_before.wait_recv()
    to_up.wait_recv()
    to_down.wait_recv()
    field[pl.ds(MARGIN - 1, full, stride=pitch), :] = halo[0].astype(F32)
    field[pl.ds(MARGIN + rows, full, stride=pitch), :] = halo[1].astype(F32)

    @pl.when(my > 0)
    def _():
        edge_f[0] = edge_in[0].astype(F32)

    @pl.when(my == 0)
    def _():
        edge_f[0] = jnp.zeros((2, rows, cells), F32)

    @pl.when(my < ny - 1)
    def _():
        edge_f[1] = edge_in[1].astype(F32)

    @pl.when(my == ny - 1)
    def _():
        edge_f[1] = jnp.zeros((2, rows, cells), F32)

    for f in range(2):
        for u in range(units):
            def local(z, carry):
                j = u * layers + z
                q = f * slab + j
                here = field[middle(q), :]
                south = jnp.where(
                    lane == 0, pltpu.roll(edge_f[0, f], lax.rem(cells - j, cells), 1),
                    pltpu.roll(here, 1, 1),
                )
                north = jnp.where(
                    lane == cells - 1, pltpu.roll(edge_f[1, f], cells - 1 - j, 1),
                    pltpu.roll(here, cells - 1, 1),
                )
                near = field[pl.ds(q * pitch + MARGIN - 1, rows), :]
                near = near + field[pl.ds(q * pitch + MARGIN + 1, rows), :]
                value = kappa_ref[u] * (near + south + north - 4.0 * here)
                for w in range(units):
                    value = value + blocks_ref[units * u + w].astype(F32) * field[
                        middle(f * slab + w * layers + z), :
                    ]
                before_image[q] = value
                return carry

            lax.fori_loop(0, layers, local, 0)

    def insert(x, carry):
        back[pl.ds(x, full, stride=rows), :] = coupled[x].astype(F32)
        return carry

    for c in range(chunks):
        for k in order:
            backward_in(c, k).wait_recv()

        def chunk_row(i, carry):
            return insert(lax.div(i, step) * group + c * step + lax.rem(i, step), carry)

        lax.fori_loop(0, nz * step, chunk_row, 0, unroll=2)

    def image(j, carry):
        ba, be = carry
        b = b_ref[j].astype(F32)
        images = []
        for f in range(2):
            q = f * slab + j
            coup = back[pl.ds(pl.multiple_of(q * rows, 8), rows), :]
            images.append(ocean * (coup + before_image[q]))
            outs[f][j] = images[f].astype(BF16)
        return ba + b * images[0], be + b * images[1]

    pair = lax.fori_loop(0, slab, image, (zero, zero), unroll=2)

    lines = [jnp.sum(v, axis=0, keepdims=True) for v in (*sums, *pair)]
    value = jnp.concatenate(lines + [jnp.zeros((3, cells), F32)], axis=0)
    base = 0
    stages = (
        ("lz", mz, nz, stat_z, sr_z), ("ty", my, ny, stat_y, sr_y), ("tx", mx, nx, stat_x, sr_x)
    )
    sends = []
    for s, (name, me, size, box, sem) in enumerate(stages):
        stat_out[s] = value
        box[me] = value
        for k in range(1, size):
            copy = pltpu.make_async_remote_copy(
                src_ref=stat_out.at[s], dst_ref=box.at[me], send_sem=ss.at[base + k - 1],
                recv_sem=sem.at[me], device_id={name: lax.rem(me + k, size)},
                device_id_type=MESH,
            )
            copy.start()
            sends.append(copy)
        base += size - 1
        for k in range(1, size):
            src = lax.rem(me + size - k, size)
            pltpu.make_async_remote_copy(
                src_ref=stat_out.at[s], dst_ref=box.at[src], send_sem=ss.at[0],
                recv_sem=sem.at[src], device_id={name: src}, device_id_type=MESH,
            ).wait_recv()
        value = box[0]
        for i in range(1, size):
            value = value + box[i]
    final = jnp.broadcast_to(jnp.sum(value, axis=1, keepdims=True), (8, cells))
    bb, cc, cv, ba, be = (final[i:i + 1] for i in range(5))
    line = lax.broadcasted_iota(jnp.int32, (1, cells), 1)
    top = jnp.where(line == 0, ba, jnp.where(line == 1, be, cv))
    low = jnp.where(line == 2, cc, bb)
    border_ref[...] = top / jnp.sqrt(low)

    for c in range(chunks):
        for k in order:
            forward(c, k).wait_send()
            backward(c, k).wait_send()
    to_later.wait_send()
    to_before.wait_send()
    to_up.wait_send()
    to_down.wait_send()
    for copy in sends:
        copy.wait_send()


def body(sizes, *arrays):
    nx, ny, nz = sizes
    rows, units, layers, cells = arrays[0].shape
    slab = units * layers
    full = 2 * slab
    group = rows // nz
    chunks = 4 if group % 4 == 0 else 1
    step = group // chunks
    mixes = arrays[6].shape[1]
    wide = [v.transpose(1, 2, 0, 3).reshape(slab, rows, cells) for v in arrays[:4]]
    args = (*wide, arrays[4], arrays[5].T, arrays[6].transpose(1, 0, 2), *arrays[7:])
    vmem = pl.BlockSpec(memory_space=pltpu.VMEM)
    smem = pl.BlockSpec(memory_space=pltpu.SMEM)
    hbm = pl.BlockSpec(memory_space=pl.ANY)
    dma = pltpu.SemaphoreType.DMA
    out_t, out_d, border = pl.pallas_call(
        functools.partial(kernel, sizes, chunks, units),
        out_shape=(
            jax.ShapeDtypeStruct((slab, rows, cells), BF16),
            jax.ShapeDtypeStruct((slab, rows, cells), BF16),
            jax.ShapeDtypeStruct((1, cells), F32),
        ),
        in_specs=[hbm] * 4 + [vmem] * 2 + [hbm] * 2 + [smem],
        out_specs=(vmem, vmem, vmem),
        scratch_shapes=[
            *[pltpu.VMEM((slab, rows, cells), BF16)] * 4,
            pltpu.VMEM((mixes, rows, cells), BF16),
            pltpu.VMEM(arrays[7].shape, BF16),
            pltpu.VMEM((rows, full, cells), BF16),
            pltpu.VMEM((chunks, nz, step, full, cells), BF16),
            pltpu.VMEM((chunks, nz, step, full, cells), BF16),
            pltpu.VMEM((rows, full, cells), BF16),
            pltpu.VMEM((rows, cells), F32),
            pltpu.VMEM((nz * full, nz * full), BF16),
            pltpu.VMEM((full * (rows + 2 * MARGIN), cells), F32),
            pltpu.VMEM((full * rows, cells), F32),
            pltpu.VMEM((full, rows, cells), F32),
            pltpu.VMEM((2, full, cells), BF16),
            pltpu.VMEM((2, 2, rows, cells), BF16),
            pltpu.VMEM((2, 2, rows, cells), BF16),
            pltpu.VMEM((2, 2, rows, cells), F32),
            pltpu.VMEM((3, 8, cells), F32),
            pltpu.VMEM((nz, 8, cells), F32),
            pltpu.VMEM((ny, 8, cells), F32),
            pltpu.VMEM((nx, 8, cells), F32),
            dma((6,)),
            dma((chunks, nz)),
            dma((chunks, nz)),
            dma((chunks, nz)),
            dma((chunks, nz)),
            dma((2,)),
            dma((2,)),
            dma((2,)),
            dma((2,)),
            dma((nx + ny + nz - 3,)),
            dma((nz,)),
            dma((ny,)),
            dma((nx,)),
        ],
        compiler_params=pltpu.CompilerParams(
            collective_id=0, has_side_effects=True, vmem_limit_bytes=56 * 1024 * 1024
        ),
    )(*args)
    outs = [
        v.reshape(units, layers, rows, cells).transpose(2, 0, 1, 3) for v in (out_t, out_d)
    ]
    return (*outs, border[0, :3])


def solution(mesh):
    wide = P("tx", None, "lz", "ty")
    in_specs = (
        wide, wide, wide, wide, P("tx", "ty"), P("tx", "ty"), P("tx", None, "ty"), P(), P(),
    )
    sizes = tuple(mesh.shape[name] for name in ("tx", "ty", "lz"))
    return jax.shard_map(
        functools.partial(body, sizes), mesh=mesh, in_specs=in_specs,
        out_specs=(wide, wide, P()), check_vma=False,
    )
```

time: 79 us -> 83 us (1.051)
  Pallas kernels: 69.4 us -> 78.1 us
  local copies, waits for them, and re-layouts: 8.59 us -> 3.95 us
    pallas_call x1, Pallas kernels: 69.4 us -> 78.1 us  [body(): pl.pallas_call(functools.partial(kernel, sizes, chunks, units), out_shape...]
    unnamed x22 -> x6, local copies, waits for them, and re-layouts: 8.08 us -> 3.43 us
where the time goes in v2:
time: 83 us; the launch traced here: 82.7 us
  Pallas kernels  78.1 us (94%)
  local copies, waits for them, and re-layouts  3.95 us (5%)
    pallas_call x1, Pallas kernels, body(): pl.pallas_call(functools.partial(kernel, sizes, chunks, units), out_shape...  78.1 us
    unnamed x6, local copies, waits for them, and re-layouts  3.43 us

profile of v2, /device:TPU:0, one launch (start us, length us, event | category | flops | bytes accessed | tf_op | source)
XLA Modules:
  0.0 82.7 jit_solution(1044404903866170143)
XLA Ops:
  0.6 78.1 %shard_map.112 = (bf16[72,32,128]{2,1,0:T(8,128)(2,1)}, bf16[72,32,128]{2,1,0:T(8,128)(2,1)}, f32[1,128]{1,0:T(1,128)}) custom-call(bf16[72,32,128]{2,1,0:T(8,128)(2,1)} %bitcast.24, bf16[72,32,128]{2,1,0:T(8,128)(2,1)} %bitcast.25, bf16[72,32,128]{2,1,0:T(8,128)(2,1)} %bitcast.26, bf16[72,32,128]{2,1,0:T(8,128)(2,1)} %bitcast.27, s32[32,128]{1,0:T(8,128)} %land_ref.1, ...), custom_call_target="tpu_custom_call" | custom-call | tf_op jit(solution)/shard_map/pallas_call | solution.py:357
  78.7 0.0 copy-start.1
  78.7 0.6 copy-done.1
  79.4 0.5 slice_bitcast_fusion
  79.9 0.0 copy-start
  79.9 2.0 %copy.14 = bf16[32,6,12,128]{3,0,2,1:T(8,128)(2,1)} copy(bf16[32,6,12,128]{3,0,2,1:T(8,128)(2,1)} %bitcast.23) | data formatting | bytes 1179648
  81.9 0.0 copy-done
  81.9 0.8 copy.15
Async XLA Ops:
  78.7 0.6 copy-start.1
  79.9 2.0 %copy-start = (bf16[72,32,128]{2,1,0:T(8,128)(2,1)S(1)}, bf16[72,32,128]{2,1,0:T(8,128)(2,1)}, u32[]{:S(2)}) copy-start(bf16[72,32,128]{2,1,0:T(8,128)(2,1)} %get-tuple-element.7) | copy-start | bytes 1769476

commit v3 on v2

--- a/solution.py
+++ b/solution.py
@@ -66,30 +66,21 @@
     for f in range(2):
         loads[f].wait()
 
-        def mask(j, edges):
-            first, last = edges
-            value = fields[f][j].astype(F32) * ocean
-            field[middle(f * slab + j), :] = value
-            first = jnp.where(lane == j, pltpu.roll(value, j, 1), first)
-            last = jnp.where(lane == j, pltpu.roll(value, j + 1, 1), last)
-            return first, last
-
-        blank = jnp.zeros((rows, cells), F32)
-        first, last = lax.fori_loop(0, slab, mask, (blank, blank), unroll=2)
-        edge_out[0, f] = first.astype(BF16)
-        edge_out[1, f] = last.astype(BF16)
-
-    def pack(x, carry):
-        masked[x] = field[pl.ds(MARGIN + x, full, stride=pitch), :].astype(BF16)
-        return carry
-
-    lax.fori_loop(0, rows, pack, 0, unroll=2)
-
-    def own_row(i, carry):
-        arrived[lax.div(i, step), mz, lax.rem(i, step)] = masked[mz * group + i]
-        return carry
-
-    lax.fori_loop(0, group, own_row, 0)
+        def mask(j, carry):
+            field[middle(f * slab + j), :] = fields[f][j].astype(F32) * ocean
+            return carry
+
+        lax.fori_loop(0, slab, mask, 0, unroll=8)
+
+    def pack(c):
+        def pack_row(i, carry):
+            x = lax.div(i, step) * group + c * step + lax.rem(i, step)
+            masked[x] = field[pl.ds(MARGIN + x, full, stride=pitch), :].astype(BF16)
+            return carry
+
+        lax.fori_loop(0, nz * step, pack_row, 0, unroll=4)
+
+    pack(0)
 
     pl.semaphore_wait(barrier, (nx - 1) + (ny - 1) + (nz - 1))
 
@@ -138,8 +129,18 @@
         )
 
     order = sorted(range(1, nz), key=lambda k: -min(k, nz - k))
+    for c in range(1, chunks):
+        pack(c)
+        for k in order:
+            forward(c - 1, k).start()
+
+    def own_row(i, carry):
+        arrived[lax.div(i, step), mz, lax.rem(i, step)] = masked[mz * group + i]
+        return carry
+
+    lax.fori_loop(0, group, own_row, 0)
     for k in order:
-        forward(0, k).start()
+        forward(chunks - 1, k).start()
     later, before = lax.rem(mx + 1, nx), lax.rem(mx + nx - 1, nx)
     to_later = pltpu.make_async_remote_copy(
         src_ref=masked.at[rows - 1], dst_ref=halo.at[0], send_sem=xs.at[0], recv_sem=xr.at[0],
@@ -151,6 +152,19 @@
     )
     to_later.start()
     to_before.start()
+    for f in range(2):
+        def edges(j, carry):
+            first, last = carry
+            value = field[middle(f * slab + j), :]
+            first = jnp.where(lane == j, pltpu.roll(value, j, 1), first)
+            last = jnp.where(lane == j, pltpu.roll(value, j + 1, 1), last)
+            return first, last
+
+        blank = jnp.zeros((rows, cells), F32)
+        first, last = lax.fori_loop(0, slab, edges, (blank, blank), unroll=4)
+        edge_out[0, f] = first.astype(BF16)
+        edge_out[1, f] = last.astype(BF16)
+
     up, down = lax.rem(my + 1, ny), lax.rem(my + ny - 1, ny)
     to_up = pltpu.make_async_remote_copy(
         src_ref=edge_out.at[1], dst_ref=edge_in.at[0], send_sem=ys.at[0], recv_sem=yr.at[0],
@@ -160,12 +174,6 @@
         src_ref=edge_out.at[0], dst_ref=edge_in.at[1], send_sem=ys.at[1], recv_sem=yr.at[1],
         device_id={"ty": down}, device_id_type=MESH,
     )
-    to_up.start()
-    to_down.start()
-    for c in range(1, chunks):
-        for k in order:
-            forward(c, k).start()
-
     col = units * layers * nz
     wide = nz * full
 
@@ -188,6 +196,8 @@
         both = jnp.dot(left, chooser((col, wide), 1, f), preferred_element_type=F32)
         total = both if total is None else total + both
     big_k[...] = total.astype(BF16)
+    to_up.start()
+    to_down.start()
 
     for load in loads[3:]:
         load.wait()
@@ -211,7 +221,7 @@
         for d in range(nz):
             for r in range(step):
                 product[c, d, r] = result[d * full:(d + 1) * full, r * cells:(r + 1) * cells]
-        sums = lax.fori_loop(c * quarter, (c + 1) * quarter, norms, sums)
+        sums = lax.fori_loop(c * quarter, (c + 1) * quarter, norms, sums, unroll=2)
         for k in order:
             backward(c, k).start()
         for r in range(step):
@@ -264,7 +274,7 @@
                 before_image[q] = value
                 return carry
 
-            lax.fori_loop(0, layers, local, 0)
+            lax.fori_loop(0, layers, local, 0, unroll=2)
 
     def insert(x, carry):
         back[pl.ds(x, full, stride=rows), :] = coupled[x].astype(F32)
@@ -277,7 +287,7 @@
         def chunk_row(i, carry):
             return insert(lax.div(i, step) * group + c * step + lax.rem(i, step), carry)
 
-        lax.fori_loop(0, nz * step, chunk_row, 0, unroll=2)
+        lax.fori_loop(0, nz * step, chunk_row, 0, unroll=4)
 
     def image(j, carry):
         ba, be = carry
@@ -290,7 +300,7 @@
             outs[f][j] = images[f].astype(BF16)
         return ba + b * images[0], be + b * images[1]
 
-    pair = lax.fori_loop(0, slab, image, (zero, zero), unroll=2)
+    pair = lax.fori_loop(0, slab, image, (zero, zero), unroll=6)
 
     lines = [jnp.sum(v, axis=0, keepdims=True) for v in (*sums, *pair)]
     value = jnp.concatenate(lines + [jnp.zeros((3, cells), F32)], axis=0)
@@ -399,7 +409,7 @@
             dma((nx,)),
         ],
         compiler_params=pltpu.CompilerParams(
-            collective_id=0, has_side_effects=True, vmem_limit_bytes=56 * 1024 * 1024
+            collective_id=0, has_side_effects=True, vmem_limit_bytes=52 * 1024 * 1024
         ),
     )(*args)
     outs = [

time: 83 us -> 74.2 us (0.89)
  Pallas kernels: 78.1 us -> 67.8 us
  local copies, waits for them, and re-layouts: 3.95 us -> 5.41 us
    pallas_call x1, Pallas kernels: 78.1 us -> 67.8 us  [body(): pl.pallas_call(functools.partial(kernel, sizes, chunks, units), out_shape...]
    unnamed x6 -> x12, local copies, waits for them, and re-layouts: 3.43 us -> 4.9 us
where the time goes in v3:
time: 74.2 us; the launch traced here: 73.9 us
  Pallas kernels  67.8 us (91%)
  local copies, waits for them, and re-layouts  5.41 us (7%)
    pallas_call x1, Pallas kernels, body(): pl.pallas_call(functools.partial(kernel, sizes, chunks, units), out_shape...  67.8 us
    unnamed x12, local copies, waits for them, and re-layouts  4.9 us

profile of v3, /device:TPU:0, one launch (start us, length us, event | category | flops | bytes accessed | tf_op | source)
XLA Modules:
  0.0 73.9 jit_solution(8078787386822267399)
XLA Ops:
  0.6 0.0 copy-start.3
  0.6 0.0 copy-start.4
  0.7 0.6 copy-done.3
  1.3 0.0 copy-done.4
  1.3 0.0 copy-start
  1.3 1.0 %copy-done = bf16[32,36,128]{2,0,1:T(8,128)(2,1)S(1)} copy-done((bf16[32,36,128]{2,0,1:T(8,128)(2,1)S(1)}, bf16[32,36,128]{2,0,1:T(8,128)(2,1)}, u32[]{:S(2)}) %copy-start) | copy-done | bytes 294936
  2.3 0.0 copy-start.1
  2.3 0.9 %copy-done.1 = bf16[288,288]{1,0:T(8,128)(2,1)S(1)} copy-done((bf16[288,288]{1,0:T(8,128)(2,1)S(1)}, bf16[288,288]{1,0:T(8,128)(2,1)}, u32[]{:S(2)}) %copy-start.1) | copy-done | bytes 165912
  3.2 0.0 copy-start.2
  3.2 0.7 copy-done.2
  3.9 67.8 %shard_map.112 = (bf16[72,32,128]{2,1,0:T(8,128)(2,1)S(1)}, bf16[72,32,128]{2,1,0:T(8,128)(2,1)S(1)}, f32[1,128]{1,0:T(1,128)S(1)}) custom-call(bf16[72,32,128]{2,1,0:T(8,128)(2,1)} %bitcast.26, bf16[72,32,128]{2,1,0:T(8,128)(2,1)} %bitcast.27, bf16[72,32,128]{2,1,0:T(8,128)(2,1)} %bitcast.28, bf16[72,32,128]{2,1,0:T(8,128)(2,1)} %bitcast.29, ...), custom_call_target="tpu_custom_call" | custom-call | tf_op jit(solution)/shard_map/pallas_call | solution.py:367
  71.8 0.5 slice_bitcast_fusion
  72.3 0.8 %copy.14 = bf16[32,6,12,128]{3,0,2,1:T(8,128)(2,1)} copy(bf16[32,6,12,128]{3,0,2,1:T(8,128)(2,1)S(1)} %bitcast.23) | data formatting | bytes 1179648
  73.1 0.8 %copy.15 = bf16[32,6,12,128]{3,0,2,1:T(8,128)(2,1)} copy(bf16[32,6,12,128]{3,0,2,1:T(8,128)(2,1)S(1)} %bitcast.22) | data formatting | bytes 1179648
Async XLA Ops:
  0.6 0.7 copy-start.3
  0.6 0.7 copy-start.4
  1.3 1.0 %copy-start = (bf16[32,36,128]{2,0,1:T(8,128)(2,1)S(1)}, bf16[32,36,128]{2,0,1:T(8,128)(2,1)}, u32[]{:S(2)}) copy-start(bf16[32,36,128]{2,0,1:T(8,128)(2,1)} %param.15) | copy-start | bytes 884740
  2.3 0.9 %copy-start.1 = (bf16[288,288]{1,0:T(8,128)(2,1)S(1)}, bf16[288,288]{1,0:T(8,128)(2,1)}, u32[]{:S(2)}) copy-start(bf16[288,288]{1,0:T(8,128)(2,1)} %k_hbm.1) | copy-start | bytes 497668
  3.2 0.7 copy-start.2

commit v4 on v3

--- a/solution.py
+++ b/solution.py
@@ -20,8 +20,8 @@
     out_t, out_d, border_ref,
     test_ref, dir_ref, b_ref, c_ref, blocks_ref, k_ref,
     masked, arrived, product, coupled, weight, big_k, field, back, before_image, halo,
-    edge_out, edge_in, edge_f, stat_out, stat_z, stat_y, stat_x,
-    ls, fs, fr, bs, br, xs, xr, ys, yr, ss, sr_z, sr_y, sr_x,
+    edge_out, edge_in, edge_f, stat_out, stat_z, stat_y,
+    ls, fs, fr, bs, br, xs, xr, ys, yr, ss, sr_z, sr_y,
 ):
     nx, ny, nz = sizes
     slab, rows, cells = test_ref.shape
@@ -45,11 +45,13 @@
         load.start()
 
     barrier = pltpu.get_barrier_semaphore()
-    for name, me, size in (("tx", mx, nx), ("ty", my, ny), ("lz", mz, nz)):
-        for k in range(1, size):
-            pl.semaphore_signal(
-                barrier, inc=1, device_id={name: lax.rem(me + k, size)}, device_id_type=MESH
-            )
+    for k in range(1, nz):
+        pl.semaphore_signal(
+            barrier, inc=1, device_id={"lz": lax.rem(mz + k, nz)}, device_id_type=MESH
+        )
+    for k in range(1, nx * ny):
+        near = {"ty": lax.rem(my + k // nx, ny), "tx": lax.rem(mx + k % nx, nx)}
+        pl.semaphore_signal(barrier, inc=1, device_id=near, device_id_type=MESH)
 
     lane = lax.broadcasted_iota(jnp.int32, (rows, cells), 1)
     line = lax.broadcasted_iota(jnp.int32, (rows, rows), 0)
@@ -82,7 +84,7 @@
 
     pack(0)
 
-    pl.semaphore_wait(barrier, (nx - 1) + (ny - 1) + (nz - 1))
+    pl.semaphore_wait(barrier, nx * ny + nz - 2)
 
     def forward(c, k):
         to = lax.rem(mz + k, nz)
@@ -305,27 +307,31 @@
     lines = [jnp.sum(v, axis=0, keepdims=True) for v in (*sums, *pair)]
     value = jnp.concatenate(lines + [jnp.zeros((3, cells), F32)], axis=0)
     base = 0
+    plane = [(i, k) for i in range(ny) for k in range(nx)]
     stages = (
-        ("lz", mz, nz, stat_z, sr_z), ("ty", my, ny, stat_y, sr_y), ("tx", mx, nx, stat_x, sr_x)
+        ([{"lz": lax.rem(mz + k, nz)} for k in range(nz)], nz, stat_z, sr_z, mz,
+         [lax.rem(mz + nz - k, nz) for k in range(nz)]),
+        ([{"ty": lax.rem(my + i, ny), "tx": lax.rem(mx + k, nx)} for i, k in plane],
+         ny * nx, stat_y, sr_y, my * nx + mx,
+         [lax.rem(my + ny - i, ny) * nx + lax.rem(mx + nx - k, nx) for i, k in plane]),
     )
     sends = []
-    for s, (name, me, size, box, sem) in enumerate(stages):
+    for s, (peers, size, box, sem, me, sources) in enumerate(stages):
         stat_out[s] = value
         box[me] = value
         for k in range(1, size):
             copy = pltpu.make_async_remote_copy(
                 src_ref=stat_out.at[s], dst_ref=box.at[me], send_sem=ss.at[base + k - 1],
-                recv_sem=sem.at[me], device_id={name: lax.rem(me + k, size)},
-                device_id_type=MESH,
+                recv_sem=sem.at[me], device_id=peers[k], device_id_type=MESH,
             )
             copy.start()
             sends.append(copy)
         base += size - 1
         for k in range(1, size):
-            src = lax.rem(me + size - k, size)
+            src = sources[k]
             pltpu.make_async_remote_copy(
                 src_ref=stat_out.at[s], dst_ref=box.at[src], send_sem=ss.at[0],
-                recv_sem=sem.at[src], device_id={name: src}, device_id_type=MESH,
+                recv_sem=sem.at[src], device_id=peers[k], device_id_type=MESH,
             ).wait_recv()
         value = box[0]
         for i in range(1, size):
@@ -360,6 +366,7 @@
     mixes = arrays[6].shape[1]
     wide = [v.transpose(1, 2, 0, 3).reshape(slab, rows, cells) for v in arrays[:4]]
     args = (*wide, arrays[4], arrays[5].T, arrays[6].transpose(1, 0, 2), *arrays[7:])
+    args = (*[pltpu.with_memory_space_constraint(v, pltpu.HBM) for v in args[:8]], args[8])
     vmem = pl.BlockSpec(memory_space=pltpu.VMEM)
     smem = pl.BlockSpec(memory_space=pltpu.SMEM)
     hbm = pl.BlockSpec(memory_space=pl.ANY)
@@ -390,10 +397,9 @@
             pltpu.VMEM((2, 2, rows, cells), BF16),
             pltpu.VMEM((2, 2, rows, cells), BF16),
             pltpu.VMEM((2, 2, rows, cells), F32),
-            pltpu.VMEM((3, 8, cells), F32),
+            pltpu.VMEM((2, 8, cells), F32),
             pltpu.VMEM((nz, 8, cells), F32),
-            pltpu.VMEM((ny, 8, cells), F32),
-            pltpu.VMEM((nx, 8, cells), F32),
+            pltpu.VMEM((ny * nx, 8, cells), F32),
             dma((6,)),
             dma((chunks, nz)),
             dma((chunks, nz)),
@@ -403,10 +409,9 @@
             dma((2,)),
             dma((2,)),
             dma((2,)),
-            dma((nx + ny + nz - 3,)),
+            dma((nx * ny + nz - 2,)),
             dma((nz,)),
-            dma((ny,)),
-            dma((nx,)),
+            dma((ny * nx,)),
         ],
         compiler_params=pltpu.CompilerParams(
             collective_id=0, has_side_effects=True, vmem_limit_bytes=52 * 1024 * 1024

time: 74.2 us -> 70.7 us (0.953)
  local copies, waits for them, and re-layouts: 5.41 us -> 2.79 us
  Pallas kernels: 67.8 us -> 67 us
    unnamed x12 -> x4, local copies, waits for them, and re-layouts: 4.9 us -> 2.28 us
    pallas_call x1, Pallas kernels: 67.8 us -> 67 us  [body(): pl.pallas_call(functools.partial(kernel, sizes, chunks, units), out_shape...]
where the time goes in v4:
time: 70.7 us; the launch traced here: 70.5 us
  Pallas kernels  67 us (95%)
  local copies, waits for them, and re-layouts  2.79 us (4%)
    pallas_call x1, Pallas kernels, body(): pl.pallas_call(functools.partial(kernel, sizes, chunks, units), out_shape...  67 us
    unnamed x4, local copies, waits for them, and re-layouts  2.28 us

profile of v4, /device:TPU:0, one launch (start us, length us, event | category | flops | bytes accessed | tf_op | source)
XLA Modules:
  0.0 70.5 jit_solution(168517238880081409)
XLA Ops:
  0.6 0.0 copy-start
  0.6 0.6 copy-done
  1.3 67.0 %shard_map.112 = (bf16[72,32,128]{2,1,0:T(8,128)(2,1)S(1)}, bf16[72,32,128]{2,1,0:T(8,128)(2,1)S(1)}, f32[1,128]{1,0:T(1,128)S(1)}) custom-call(bf16[72,32,128]{2,1,0:T(8,128)(2,1)} %bitcast.24, bf16[72,32,128]{2,1,0:T(8,128)(2,1)} %bitcast.25, bf16[72,32,128]{2,1,0:T(8,128)(2,1)} %bitcast.26, bf16[72,32,128]{2,1,0:T(8,128)(2,1)} %bitcast.27, ...), custom_call_target="tpu_custom_call" | custom-call | tf_op jit(solution)/shard_map/pallas_call | solution.py:374
  68.3 0.5 slice_bitcast_fusion
  68.8 0.8 %copy.14 = bf16[32,6,12,128]{3,0,2,1:T(8,128)(2,1)} copy(bf16[32,6,12,128]{3,0,2,1:T(8,128)(2,1)S(1)} %bitcast.23) | data formatting | bytes 1179648
  69.7 0.8 %copy.15 = bf16[32,6,12,128]{3,0,2,1:T(8,128)(2,1)} copy(bf16[32,6,12,128]{3,0,2,1:T(8,128)(2,1)S(1)} %bitcast.22) | data formatting | bytes 1179648
Async XLA Ops:
  0.6 0.7 copy-start
